TPU v7x, 32 devices: a whole 2x2x4 slice. The times are simulated.
32 devices in a mesh: parts: 2 (over y), row: 4 (over x, core), col: 4 (over z).
Axes of the slice: x: 2, y: 2, z: 4, core: 2. Of those that a mesh axis runs over, the one named last changes fastest.
Arguments:
- left_factor: bfloat16 [6144, 8, 1024], P(('parts', 'col'), None, 'row'), parts along dimension 0, may hold values from -0.109375 to 0.109375
- right_factor: bfloat16 [64, 1024, 3072], P('parts', 'col', 'row'), parts along dimension 0, may hold values from -6 to 6
- amplitudes: bfloat16 [1024, 1024, 512], P('row', 'col', 'parts'), parts along dimension 2, may hold values from -0.0078125 to 0.0078125
Outputs:
- ladder: float32 [512, 256], P(('parts', 'row', 'col')), parts along dimension 0
There are 2 independent parts, one for each index of `parts`. A program takes and returns all parts, laid end to end along the dimension named above; each array names one. Nothing has to cross between parts.
All inputs are finite; a program needn't handle non-finite values.
Results may differ from a plain program's by a relative error of at most 0.0029.
Values may be sent and summed in bfloat16 or wider, within the bound.
A program may use at most 192 MiB of HBM per device.

v0:
```python
import jax
import jax.numpy as jnp
from jax import lax
from jax.sharding import PartitionSpec as P


def contract_aux(left_rows, right_rows):
    return lax.dot_general(
        left_rows, right_rows, (((0,), (1,)), ((), ())), preferred_element_type=jnp.float32
    )


def on_device(left_factor, right_factor, amplitudes):
    width_a = left_factor.shape[1]
    span_c = left_factor.shape[2]
    width_b = right_factor.shape[0]
    span_d = right_factor.shape[1]
    pair_count = amplitudes.shape[2]
    left_all = lax.all_gather(left_factor, "col", axis=0, tiled=True)
    left_flat = left_all.reshape(left_all.shape[0], width_a * span_c)
    shard_part = lax.all_gather(right_factor, "row", axis=2, tiled=True)
    length = shard_part.shape[2]
    integral = contract_aux(left_flat, shard_part.reshape(width_b * span_d, length))
    rounded = integral.astype(jnp.bfloat16).reshape(width_a, span_c, width_b, span_d)
    partial_sums = jnp.einsum(
        "cdp,acbd->pab", amplitudes, rounded, preferred_element_type=jnp.float32
    ).reshape(pair_count, width_a * width_b)
    return lax.psum_scatter(partial_sums, ("row", "col"), scatter_dimension=0, tiled=True)


def solution(mesh):
    return jax.shard_map(
        on_device,
        mesh=mesh,
        in_specs=(
            P(("parts", "col"), None, "row"),
            P("parts", "col", "row"),
            P("row", "col", "parts"),
        ),
        out_specs=P(("parts", "row", "col"), None),
        check_vma=False,
    )
```

profile of v0, /device:TPU:0, one launch (start us, length us, event | category | flops | bytes accessed | tf_op | source)
XLA Modules:
  0.0 753.3 jit_solution(4722424935364290025)
XLA Ops:
  6.5 0.0 all-gather.3.cloned.1.call-start
  6.5 0.7 all-gather.3.cloned.1.call-update
  7.3 0.0 all-gather.5.cloned.1.call-start
  7.3 0.7 all-gather.5.cloned.1.call-update
  8.0 0.0 reduce-scatter.2.cloned.1.call-start
  8.1 221.8 %all-gather.3.cloned.1.call-done = bf16[3072,8,256]{2,1,0:T(8,128)(2,1)} async-done(((bf16[768,8,256]{2,1,0:T(8,128)(2,1)}), bf16[3072,8,256]{2,1,0:T(8,128)(2,1)}) %all-gather.3.cloned.1.call-update) | async-done | bytes 12582928 | tf_op jit(solution)/shard_map/all_gather | solution.py:19
  229.8 13.5 %copy.7 = bf16[384,8,8,256]{3,1,2,0:T(8,128)(2,1)} copy(bf16[384,8,8,256]{3,2,1,0:T(8,128)(2,1)} %bitcast.23) | data formatting | bytes 25165824
  243.3 285.9 %all-gather.5.cloned.1.call-done = bf16[32,256,3072]{2,1,0:T(8,128)(2,1)} async-done(((bf16[32,256,768]{2,1,0:T(8,128)(2,1)}), bf16[32,256,3072]{2,1,0:T(8,128)(2,1)}) %all-gather.5.cloned.1.call-update) | async-done | bytes 50331664 | tf_op jit(solution)/shard_map/all_gather | solution.py:21
  529.2 115.1 %convolution_convert_fusion = bf16[2048,8192]{1,0:T(8,128)(2,1)} fusion(bf16[3072,2048]{1,0:T(8,128)(2,1)} %bitcast.24, bf16[8192,3072]{1,0:T(8,128)(2,1)} %bitcast.26), kind=kOutput, calls=%fused_computation.3 | convolution fusion | flops 103095992320 | bytes 96468992 | tf_op jit(solution)/shard_map/dot_general | solution.py:8
  644.3 23.0 %copy.8 = bf16[256,8,32,256]{3,2,1,0:T(8,128)(2,1)} copy(bf16[256,8,32,256]{3,1,2,0:T(8,128)(2,1)} %bitcast.22) | data formatting | bytes 67108864
  667.3 22.7 %fusion = f32[8,32,256,1]{2,1,3,0:T(8,128)S(1)} fusion(bf16[256,256,256]{2,1,0:T(8,128)(2,1)} %param.5, bf16[8,256,32,256]{3,2,1,0:T(8,128)(2,1)} %bitcast.21), kind=kOutput, calls=%fused_computation | convolution fusion | flops 8589934592 | bytes 67371008 | tf_op jit(solution)/shard_map/cdp,acbd->pab/dot_general | solution.py:25
  690.0 0.8 copy.5
  690.9 0.0 reduce-scatter.2.cloned.1.call-update
  690.9 55.9 %reduce-scatter.2.cloned.1.call-done = f32[16,256]{1,0:T(8,128)} async-done(((f32[256,256]{1,0:T(8,128)}), f32[16,256]{1,0:T(8,128)}) %reduce-scatter.2.cloned.1.call-update) | async-done | bytes 16400 | tf_op jit(solution)/shard_map/reduce_scatter | solution.py:28
Async XLA Ops:
  6.5 223.3 %all-gather.3.cloned.1.call-start = ((), (), s32[]{:S(2)}) async-start(), calls=%async_computation.1 | async-start | bytes 15728640 | tf_op jit(solution)/shard_map/all_gather | solution.py:19
  7.3 521.9 %all-gather.5.cloned.1.call-start = ((), (), s32[]{:S(2)}) async-start(), calls=%async_computation.2 | async-start | bytes 62914560 | tf_op jit(solution)/shard_map/all_gather | solution.py:21
  8.0 738.8 %reduce-scatter.2.cloned.1.call-start = ((), (), s32[]{:S(2)}) async-start(), calls=%async_computation.3 | async-start | bytes 278528 | tf_op jit(solution)/shard_map/reduce_scatter | solution.py:28
Sparse Core Ops, SparseCore 0:
  8.9 220.8 all-gather.2
  231.4 297.7 all-gather.4
  691.0 55.7 reduce-scatter.1
where the time goes:
time: 754 us; the launch traced here: 753 us
  waiting for transfers between devices  565 us (75%)
  matrix products  138 us (18%)
  local copies, waits for them, and re-layouts  37.4 us (5%)
  between operations  13.1 us (2%)
    all_gather x1, waiting for transfers between devices, on_device(): shard_part = lax.all_gather(right_factor, 'row', axis=2, tiled=True)  286 us
    all_gather x1, waiting for transfers between devices, on_device(): left_all = lax.all_gather(left_factor, 'col', axis=0, tiled=True)  222 us
    dot_general x1, matrix products, contract_aux(): lax.dot_general(left_rows, right_rows, (((0,), (1,)), ((), ())), preferre...  115 us
    reduce_scatter x1, waiting for transfers between devices, on_device(): lax.psum_scatter(partial_sums, ('row', 'col'), scatter_dimension=0, tiled...  55.9 us
    unnamed x2, local copies, waits for them, and re-layouts  36.5 us
    dot_general x1, matrix products, on_device(): jnp.einsum('cdp,acbd->pab', amplitudes, rounded, preferred_element_type=j...  22.7 us
  transfers between devices with their start and end apart: 3, of which 3 were waited for; matrix products, arithmetic and copies ran while one was open for 2% of the time, Pallas kernels for 0%

commit v1 on v0

v1 whole, which is shorter than its diff:
```python
import functools

import jax
import jax.numpy as jnp
from jax import lax
from jax.experimental import pallas as pl
from jax.experimental.pallas import tpu as pltpu
from jax.sharding import PartitionSpec as P

MESH = pl.DeviceIdType.MESH
HALVES = 2
GROUP = 8
C_STEP = 8
ROW_TILE = 512


def ladder_kernel(
    n_row, n_col, left_ref, right_ref, amp_ref, out_ref, others_ref,
    left_all, right_buf, integral, amp_buf, total, total_t, row_in, row_sum, col_in,
    own_sem, load_sem, amp_sem, l_send, l_recv, x_send, x_recv, s_send, s_recv, f_send, f_recv,
    r1_send, r1_recv, r2_send, r2_recv,
):
    rows_all, aux = left_ref.shape
    width_b, span_d, _ = right_ref.shape
    span_c, _, pairs = amp_ref.shape
    width_a = rows_all // span_c
    part_rows = rows_all // HALVES
    groups = width_b // GROUP
    r = lax.axis_index("row")
    k = lax.axis_index("col")
    mate = r + 1 - 2 * lax.rem(r, 2)
    across = lax.rem(r + 2, 4)
    diagonal = 3 - r

    barrier = pltpu.get_barrier_semaphore()
    for step in range(1, n_row):
        pl.semaphore_signal(barrier, inc=1, device_id={"row": lax.rem(r + step, n_row)}, device_id_type=MESH)
    for step in range(1, n_col):
        pl.semaphore_signal(barrier, inc=1, device_id={"col": lax.rem(k + step, n_col)}, device_id_type=MESH)
    pl.semaphore_wait(barrier, n_row + n_col - 2)

    def columns(q):
        return pl.ds(pl.multiple_of(q * aux, 128), aux)

    def left_copy(part, source, way, own):
        rows = pl.ds(part * part_rows, part_rows)
        place = left_all.at[rows, columns(source)]
        return pltpu.make_async_remote_copy(
            src_ref=left_ref.at[rows] if own else place,
            dst_ref=place,
            send_sem=l_send.at[part, source, way],
            recv_sem=l_recv.at[part, source],
            device_id={"col": k + 1 - 2 * way},
            device_id_type=MESH,
        )

    def left_own(part, act):
        @pl.when(k + 1 < n_col)
        def _():
            act(left_copy(part, k, 0, True))

        @pl.when(k >= 1)
        def _():
            act(left_copy(part, k, 1, True))

    def left_step(part, step):
        @pl.when(k >= step)
        def _():
            left_copy(part, k - step, 0, False).wait_recv()

            @pl.when(k + 1 < n_col)
            def _():
                left_copy(part, k - step, 0, False).start()

        @pl.when(k + step < n_col)
        def _():
            left_copy(part, k + step, 1, False).wait_recv()

            @pl.when(k >= 1)
            def _():
                left_copy(part, k + step, 1, False).start()

    def left_drain(part, step):
        @pl.when((k >= step) & (k + 1 < n_col))
        def _():
            left_copy(part, k - step, 0, False).wait_send()

        @pl.when((k + step < n_col) & (k >= 1))
        def _():
            left_copy(part, k + step, 1, False).wait_send()

    def mate_copy(b):
        return pltpu.make_async_remote_copy(
            src_ref=right_ref.at[b], dst_ref=others_ref.at[0, b], send_sem=s_send.at[b],
            recv_sem=s_recv.at[b], device_id={"row": mate}, device_id_type=MESH)

    def across_copy(b):
        return pltpu.make_async_remote_copy(
            src_ref=right_ref.at[b], dst_ref=others_ref.at[1, b], send_sem=x_send.at[b],
            recv_sem=x_recv.at[b], device_id={"row": across}, device_id_type=MESH)

    def onward_copy(b):
        return pltpu.make_async_remote_copy(
            src_ref=others_ref.at[1, b], dst_ref=others_ref.at[2, b], send_sem=f_send.at[b],
            recv_sem=f_recv.at[b], device_id={"row": mate}, device_id_type=MESH)

    def forward(b):
        across_copy(b).wait_recv()
        onward_copy(b).start()

    def settle(b):
        mate_copy(b).wait_recv()
        onward_copy(b).wait_recv()

    def loads(b, slot):
        sources = ((right_ref.at[b], r), (others_ref.at[0, b], mate), (others_ref.at[1, b], across), (others_ref.at[2, b], diagonal))
        return [
            pltpu.make_async_copy(source, right_buf.at[slot, :, columns(q)], load_sem.at[slot, x])
            for x, (source, q) in enumerate(sources)
        ]

    def load_start(b, slot):
        for copy in loads(b, slot):
            copy.start()

    def load_wait(b, slot):
        for copy in loads(b, slot):
            copy.wait()

    def amp_copy(c, slot):
        return pltpu.make_async_copy(amp_ref.at[pl.ds(c, C_STEP)], amp_buf.at[slot], amp_sem.at[slot])

    def contract(bi, slot, first_row, row_count):
        def tile(n, _):
            at = pl.multiple_of(n * ROW_TILE, ROW_TILE)
            integral[bi, pl.ds(at, ROW_TILE), :] = lax.dot_general(
                left_all[pl.ds(pl.multiple_of(first_row + at, ROW_TILE), ROW_TILE), :], right_buf[slot],
                (((1,), (1,)), ((), ())), preferred_element_type=jnp.float32)
            return 0

        lax.fori_loop(0, row_count // ROW_TILE, tile, 0)

    def unit(part, parts, group, first, forward_from=None, forward_count=0, done=0):
        first_row = part * part_rows
        row_count = parts * part_rows
        c_start = first_row // width_a
        blocks = row_count // width_a // C_STEP
        amp_copy(c_start, 0).start()
        base = group * GROUP
        if first:
            def body(bi, _):
                b = base + bi
                slot = lax.rem(bi, 2)

                @pl.when(bi >= done)
                def _():
                    forward(b)

                settle(b)
                load_start(b, slot)
                load_wait(b, slot)
                contract(bi, slot, first_row, row_count)
                return 0
        else:
            load_start(base, 0)

            def body(bi, _):
                slot = lax.rem(bi, 2)
                load_wait(base + bi, slot)

                @pl.when(bi + 1 < GROUP)
                def _():
                    load_start(base + bi + 1, 1 - slot)

                if forward_count:
                    every = GROUP // forward_count

                    @pl.when(lax.rem(bi, every) == every - 1)
                    def _():
                        forward(forward_from + bi // every)

                contract(bi, slot, first_row, row_count)
                return 0

        lax.fori_loop(0, GROUP, body, 0)
        group_rows = pl.ds(group * GROUP * width_a, GROUP * width_a)

        def close(n, _):
            slot = lax.rem(n, 2)
            amp_copy(c_start + n * C_STEP, slot).wait()

            @pl.when(n + 1 < blocks)
            def _():
                amp_copy(c_start + (n + 1) * C_STEP, 1 - slot).start()

            pieces = []
            for c in range(C_STEP):
                at = pl.multiple_of((n * C_STEP + c) * width_a, 8)
                piece = integral[:, pl.ds(at, width_a), :]
                pieces.append(piece.reshape(GROUP * width_a, span_d).astype(jnp.bfloat16))
            total[group_rows, :] += jnp.dot(
                jnp.concatenate(pieces, axis=1), amp_buf[slot].reshape(C_STEP * span_d, pairs),
                preferred_element_type=jnp.float32)
            return 0

        lax.fori_loop(0, blocks, close, 0)

    own_copy = pltpu.make_async_copy(left_ref, left_all.at[:, columns(k)], own_sem)
    left_own(0, lambda copy: copy.start())

    def send_right(b, _):
        across_copy(b).start()
        mate_copy(b).start()
        return 0

    lax.fori_loop(0, width_b, send_right, 0)
    own_copy.start()
    total[...] = jnp.zeros_like(total)

    steps = n_col - 1
    for step in range(1, steps + 1):
        if step == steps:
            left_own(1, lambda copy: copy.start())
        left_step(0, step)
    own_copy.wait()

    lead = groups - 1
    marks = {}
    for step in range(1, steps + 1):
        marks.setdefault(min(step, lead), []).append(step)
    for group in range(lead):
        for step in marks.get(group, []):
            left_step(1, step)
        unit(0, 1, group, True)
    for step in marks.get(lead, []):
        left_step(1, step)
    per_unit = 2
    for group in range(lead):
        unit(1, 1, group, False, lead * GROUP + group * per_unit, per_unit)
    unit(0, 2, lead, True, done=lead * per_unit)

    total_t[...] = total[...].T
    block1 = pairs // n_row

    def row_copy(q):
        return pltpu.make_async_remote_copy(
            src_ref=total_t.at[pl.ds(pl.multiple_of(q * block1, 8), block1)], dst_ref=row_in.at[r],
            send_sem=r1_send.at[q], recv_sem=r1_recv.at[r], device_id={"row": q}, device_id_type=MESH)

    def row_arrival(q):
        return pltpu.make_async_remote_copy(
            src_ref=total_t.at[pl.ds(0, block1)], dst_ref=row_in.at[q],
            send_sem=r1_send.at[q], recv_sem=r1_recv.at[q], device_id={"row": q}, device_id_type=MESH)

    for step in range(1, n_row):
        row_copy(lax.rem(r + step, n_row)).start()
    value = total_t[pl.ds(pl.multiple_of(r * block1, 8), block1), :]
    for step in range(1, n_row):
        q = lax.rem(r + step, n_row)
        row_arrival(q).wait_recv()
        value += row_in[q]
    row_sum[...] = value
    block2 = block1 // n_col

    def col_copy(q):
        return pltpu.make_async_remote_copy(
            src_ref=row_sum.at[pl.ds(pl.multiple_of(q * block2, 8), block2)], dst_ref=col_in.at[k],
            send_sem=r2_send.at[q], recv_sem=r2_recv.at[k], device_id={"col": q}, device_id_type=MESH)

    def col_arrival(q):
        return pltpu.make_async_remote_copy(
            src_ref=row_sum.at[pl.ds(0, block2)], dst_ref=col_in.at[q],
            send_sem=r2_send.at[q], recv_sem=r2_recv.at[q], device_id={"col": q}, device_id_type=MESH)

    for step in range(1, n_col):
        col_copy(lax.rem(k + step, n_col)).start()
    result = row_sum[pl.ds(pl.multiple_of(k * block2, 8), block2), :]
    for step in range(1, n_col):
        q = lax.rem(k + step, n_col)
        col_arrival(q).wait_recv()
        result += col_in[q]
    out_ref[...] = result

    for step in range(1, n_row):
        row_copy(lax.rem(r + step, n_row)).wait_send()
    for step in range(1, n_col):
        col_copy(lax.rem(k + step, n_col)).wait_send()
    for part in range(HALVES):
        left_own(part, lambda copy: copy.wait_send())
        for step in range(1, steps + 1):
            left_drain(part, step)

    def drain(b, _):
        across_copy(b).wait_send()
        mate_copy(b).wait_send()
        onward_copy(b).wait_send()
        return 0

    lax.fori_loop(0, width_b, drain, 0)


def fused(n_row, n_col, left_factor, right_factor, amplitudes):
    aux, width_a, span_c = left_factor.shape
    width_b, span_d, _ = right_factor.shape
    pairs = amplitudes.shape[2]
    rows = width_a * span_c
    left_rows = jnp.transpose(left_factor, (2, 1, 0)).reshape(rows, aux)
    anywhere = pl.BlockSpec(memory_space=pl.ANY)
    dma = pltpu.SemaphoreType.DMA
    block1 = pairs // n_row
    summed, _ = pl.pallas_call(
        functools.partial(ladder_kernel, n_row, n_col),
        out_shape=(
            jax.ShapeDtypeStruct((block1 // n_col, width_a * width_b), jnp.float32),
            jax.ShapeDtypeStruct((n_row - 1,) + right_factor.shape, jnp.bfloat16),
        ),
        in_specs=[anywhere] * 3,
        out_specs=(pl.BlockSpec(memory_space=pltpu.VMEM), anywhere),
        scratch_shapes=[
            pltpu.VMEM((rows, aux * n_col), jnp.bfloat16),
            pltpu.VMEM((2, span_d, aux * n_row), jnp.bfloat16),
            pltpu.VMEM((GROUP, rows, span_d), jnp.float32),
            pltpu.VMEM((2, C_STEP, span_d, pairs), jnp.bfloat16),
            pltpu.VMEM((width_a * width_b, pairs), jnp.float32),
            pltpu.VMEM((pairs, width_a * width_b), jnp.float32),
            pltpu.VMEM((n_row, block1, width_a * width_b), jnp.float32),
            pltpu.VMEM((block1, width_a * width_b), jnp.float32),
            pltpu.VMEM((n_col, block1 // n_col, width_a * width_b), jnp.float32),
            dma, dma((2, 4)), dma((2,)),
            dma((HALVES, n_col, 2)), dma((HALVES, n_col)),
            dma((width_b,)), dma((width_b,)), dma((width_b,)), dma((width_b,)), dma((width_b,)), dma((width_b,)),
            dma((n_row,)), dma((n_row,)), dma((n_col,)), dma((n_col,)),
        ],
        compiler_params=pltpu.CompilerParams(
            collective_id=0, has_side_effects=True, vmem_limit_bytes=60 * 1024 * 1024),
    )(left_rows, right_factor, amplitudes)
    pair_count = summed.shape[0]
    return jnp.transpose(summed.reshape(pair_count, width_b, width_a), (0, 2, 1)).reshape(pair_count, width_a * width_b)


def plain(left_factor, right_factor, amplitudes):
    aux, width_a, span_c = left_factor.shape
    width_b, span_d, _ = right_factor.shape
    left_all = lax.all_gather(left_factor, "col", axis=0, tiled=True)
    left_flat = left_all.reshape(left_all.shape[0], width_a * span_c)
    right_all = lax.all_gather(right_factor, "row", axis=2, tiled=True)
    integral = lax.dot_general(
        left_flat, right_all.reshape(width_b * span_d, right_all.shape[2]),
        (((0,), (1,)), ((), ())), preferred_element_type=jnp.float32)
    rounded = integral.astype(jnp.bfloat16).reshape(width_a, span_c, width_b, span_d)
    partial_sums = jnp.einsum(
        "cdp,acbd->pab", amplitudes, rounded, preferred_element_type=jnp.float32
    ).reshape(amplitudes.shape[2], width_a * width_b)
    return lax.psum_scatter(partial_sums, ("row", "col"), scatter_dimension=0, tiled=True)


def on_device(n_row, n_col, left_factor, right_factor, amplitudes):
    aux, width_a, span_c = left_factor.shape
    width_b, span_d, right_aux = right_factor.shape
    pairs = amplitudes.shape[2]
    fits = (
        n_row == 4 and n_col == 4 and aux == right_aux and aux % 128 == 0 and width_a % 8 == 0
        and span_d % 128 == 0 and width_b == 4 * GROUP and pairs % (8 * n_row * n_col) == 0
        and (width_a * span_c) % (HALVES * ROW_TILE) == 0 and span_c % (HALVES * C_STEP) == 0
    )
    if fits:
        return fused(n_row, n_col, left_factor, right_factor, amplitudes)
    return plain(left_factor, right_factor, amplitudes)


def solution(mesh):
    return jax.shard_map(
        functools.partial(on_device, mesh.shape["row"], mesh.shape["col"]),
        mesh=mesh,
        in_specs=(
            P(("parts", "col"), None, "row"),
            P("parts", "col", "row"),
            P("row", "col", "parts"),
        ),
        out_specs=P(("parts", "row", "col"), None),
        check_vma=False,
    )
```

time: 754 us -> 511 us (0.68)
  waiting for transfers between devices: 565 us -> 0 us
  Pallas kernels: 0 us -> 498 us
  matrix products: 138 us -> 0 us
  local copies, waits for them, and re-layouts: 37.4 us -> 7.09 us
  between operations: 13.1 us -> 0.02 us
    all_gather x2 -> x0, waiting for transfers between devices: 508 us -> none  [the longest x1 286 us: on_device(): shard_part = lax.all_gather(right_factor, 'row', axis=2, tiled=True)]
    pallas_call x0 -> x1, Pallas kernels: none -> 498 us  [fused(): pl.pallas_call(functools.partial(ladder_kernel, n_row, n_col), out_shape=...]
    dot_general x2 -> x0, matrix products: 138 us -> none  [the longest x1 115 us: contract_aux(): lax.dot_general(left_rows, right_rows, (((0,), (1,)), ((), ())), preferre...]
    reduce_scatter x1 -> x0, waiting for transfers between devices: 55.9 us -> none  [on_device(): lax.psum_scatter(partial_sums, ('row', 'col'), scatter_dimension=0, tiled...]
    unnamed x2 -> x0, local copies, waits for them, and re-layouts: 36.5 us -> none
  transfers between devices with their start and end apart: 3 -> 0, of which waited for: 3 -> 0; matrix products, arithmetic and copies ran while one was open for 2% -> 0% of each run, Pallas kernels for 0% -> 0%
where the time goes in v1:
time: 511 us; the launch traced here: 505 us
  Pallas kernels  498 us (97%)
  local copies, waits for them, and re-layouts  7.09 us (1%)
    pallas_call x1, Pallas kernels, fused(): pl.pallas_call(functools.partial(ladder_kernel, n_row, n_col), out_shape=...  498 us

profile of v1, /device:TPU:0, one launch (start us, length us, event | category | flops | bytes accessed | tf_op | source)
XLA Modules:
  0.0 504.7 jit_solution(18310607857518491332)
XLA Ops:
  0.0 5.5 %copy.8 = bf16[256,8,768]{2,1,0:T(8,128)(2,1)} copy(bf16[256,8,768]{0,1,2:T(8,128)(2,1)} %bitcast.6) | data formatting | bytes 6291456 | tf_op jit(solution)/shard_map/transpose | solution.py:307
  5.5 497.6 %shard_map.37 = (f32[16,256]{1,0:T(8,128)}, bf16[3,32,256,768]{3,2,1,0:T(8,128)(2,1)}) custom-call(bf16[2048,768]{1,0:T(8,128)(2,1)} %bitcast.5, bf16[32,256,768]{2,1,0:T(8,128)(2,1)} %right_ref.1, bf16[256,256,256]{2,1,0:T(8,128)(2,1)} %amp_ref.1), custom_call_target="tpu_custom_call" | custom-call | tf_op jit(solution)/shard_map/pallas_call | solution.py:311
  503.0 0.8 copy.9
  503.8 0.1 copy.10
  504.0 0.7 reshape.11

commit v2 on v1

--- a/solution.py
+++ b/solution.py
@@ -11,7 +11,7 @@
 HALVES = 2
 GROUP = 8
 C_STEP = 8
-ROW_TILE = 512
+ROW_TILE = 1024
 
 
 def ladder_kernel(

time: 511 us -> 497 us (0.973)
  Pallas kernels: 498 us -> 484 us
    pallas_call x1, Pallas kernels: 498 us -> 484 us  [fused(): pl.pallas_call(functools.partial(ladder_kernel, n_row, n_col), out_shape=...]
where the time goes in v2:
time: 497 us; the launch traced here: 491 us
  Pallas kernels  484 us (97%)
  local copies, waits for them, and re-layouts  7.09 us (1%)
    pallas_call x1, Pallas kernels, fused(): pl.pallas_call(functools.partial(ladder_kernel, n_row, n_col), out_shape=...  484 us

profile of v2, /device:TPU:0, one launch (start us, length us, event | category | flops | bytes accessed | tf_op | source)
XLA Modules:
  0.0 491.5 jit_solution(17854241657652311960)
XLA Ops:
  0.0 5.5 %copy.8 = bf16[256,8,768]{2,1,0:T(8,128)(2,1)} copy(bf16[256,8,768]{0,1,2:T(8,128)(2,1)} %bitcast.6) | data formatting | bytes 6291456 | tf_op jit(solution)/shard_map/transpose | solution.py:307
  5.5 484.4 %shard_map.37 = (f32[16,256]{1,0:T(8,128)}, bf16[3,32,256,768]{3,2,1,0:T(8,128)(2,1)}) custom-call(bf16[2048,768]{1,0:T(8,128)(2,1)} %bitcast.5, bf16[32,256,768]{2,1,0:T(8,128)(2,1)} %right_ref.1, bf16[256,256,256]{2,1,0:T(8,128)(2,1)} %amp_ref.1), custom_call_target="tpu_custom_call" | custom-call | tf_op jit(solution)/shard_map/pallas_call | solution.py:311
  489.8 0.8 copy.9
  490.6 0.1 copy.10
  490.8 0.7 reshape.11
